TPU v7x, 32 devices: a whole 2x2x4 slice. The times are simulated.
32 devices in a mesh: wide: 8 (over z, y), narrow: 4 (over x, core).
Axes of the slice: x: 2, y: 2, z: 4, core: 2. Of those that a mesh axis runs over, the one named last changes fastest.
Arguments:
- amplitudes: bfloat16 [256, 32768], P(('wide', 'narrow')), may hold values from -6 to 6
- integrals: bfloat16 [32768, 1024], P('wide', 'narrow'), may hold values from -0.0625 to 0.0625
- block_irrep: int32 [64], replicated, may hold values from 0 to 3
- block_units: int32 [64], replicated, may hold values from 1 to 32, 512 in all
- window_pairs: int32 [1024], replicated, may hold values from 0 to 32767
- panel_owner: int32 [4], replicated, may hold values from 0 to 3, each once
Outputs:
- ladder: bfloat16 [256, 1024], P(('wide', 'narrow'))
Inputs may be any that keep to these rules, and one draw needn't show every extreme that they name: `block_units`: the entries sum to 512; one block has exactly 32 units. `panel_owner`: each index of narrow appears once.
All inputs are finite; a program needn't handle non-finite values.
Results may differ from a plain program's by a relative error of at most 0.0017.
Values may be sent and summed in bfloat16 or wider, within the bound.
No kernel may reach another device: no remote copies, remote signals or barrier semaphores. Data moves between devices by JAX's collectives and lax.ppermute only.
A program may use at most 128 MiB of HBM per device.

v0:
```python
import jax
import jax.numpy as jnp
from jax import lax
from jax.sharding import PartitionSpec as P

UNIT = 64


def spread(value, axis, source):
    kept = jnp.where(lax.axis_index(axis) == source, value, 0).astype(value.dtype)
    return lax.psum(kept, axis)


def pair_irreps(window, block_irrep, block_units):
    block_ends = jnp.cumsum(block_units) * UNIT
    block_starts = block_ends - block_units * UNIT
    inside = (window[:, None] >= block_starts[None, :]) & (window[:, None] < block_ends[None, :])
    return jnp.sum(jnp.where(inside, block_irrep[None, :], 0), axis=1)


def on_device(amplitudes, integrals, block_irrep, block_units, window_pairs, panel_owner):
    step_count = lax.axis_size("narrow")
    local_pairs = integrals.shape[0]
    panel_width = integrals.shape[1]
    contracted = lax.axis_index("wide") * local_pairs + jnp.arange(local_pairs, dtype=jnp.int32)
    contracted_irrep = pair_irreps(contracted, block_irrep, block_units)
    transposed = lax.all_to_all(amplitudes, "wide", split_axis=1, concat_axis=0, tiled=True)

    def masked_panel(values, holder):
        window = lax.dynamic_slice_in_dim(window_pairs, holder * panel_width, panel_width)
        matches = (
            contracted_irrep[:, None] == pair_irreps(window, block_irrep, block_units)[None, :]
        )
        return jnp.where(matches, values, jnp.zeros_like(values))

    def one_panel(step_index):
        source = panel_owner[step_index]
        received = spread(integrals, "narrow", source)
        return masked_panel(received, source)

    panels_masked = [one_panel(step_index) for step_index in range(step_count)]
    return lax.psum_scatter(
        jnp.concatenate(
            [
                jnp.dot(transposed, masked, preferred_element_type=jnp.float32)
                for masked in panels_masked
            ],
            axis=1,
        ),
        "wide",
        scatter_dimension=0,
        tiled=True,
    ).astype(jnp.bfloat16)


def solution(mesh):
    placed = (P(("wide", "narrow"), None), P("wide", "narrow"), P(), P(), P(), P())
    return jax.shard_map(
        on_device,
        mesh=mesh,
        in_specs=placed,
        out_specs=P(("wide", "narrow"), None),
        check_vma=False,
    )
```

profile of v0, /device:TPU:0, one launch (start us, length us, event | category | flops | bytes accessed | tf_op | source)
XLA Modules:
  0.0 249.4 jit_solution(9631510985719156000)
XLA Ops:
  6.5 0.0 all-reduce.3.cloned.1.call-start
  6.5 1.5 fusion.29
  10.5 4.9 %broadcast_select_fusion.3 = (bf16[4096,256]{1,0:T(8,128)(2,1)}, bf16[4096,256]{1,0:T(8,128)(2,1)}, bf16[4096,256]{1,0:T(8,128)(2,1)}, bf16[4096,256]{1,0:T(8,128)(2,1)}) fusion(bf16[4096,256]{1,0:T(8,128)(2,1)} %param.7, pred[]{:T(512)S(6)} %eq.29, pred[]{:T(512)S(6)} %eq.64, pred[]{:T(512)S(6)} %eq.70, pred[]{:T(512)S(6)} %eq.67), kind=kLoop, calls=%fused_computation.15 | loop fusion | flops 4194304 | bytes 10485764 | tf_op jit(solution)/shard_map/jit(_where)/select_n | solution.py:10
  15.5 0.0 copy-start.2
  15.5 0.0 copy-start
  15.5 0.0 copy-start.1
  15.5 0.0 all-reduce.3.cloned.1.call-update
  15.5 7.5 %all-to-all-start = ((bf16[8,8,4096]{2,0,1:T(8,128)(2,1)}), bf16[8,8,4096]{2,0,1:T(8,128)(2,1)S(1)}, u32[]{:S(2)}, u32[]{:S(2)}) async-start(bf16[8,8,4096]{2,0,1:T(8,128)(2,1)} %bitcast.2), calls=%async_computation | async-start | bytes 1048576 | tf_op jit(solution)/shard_map/all_to_all | solution.py:27
  22.9 0.0 reduce-scatter.2.cloned.1.call-start
  25.5 0.0 copy-done.2
  25.5 0.1 copy.9
  25.6 0.1 reduce-window.7
  25.8 0.0 copy-done
  25.8 0.1 fusion.28
  25.9 0.1 multiply_reduce_fusion
  26.0 0.0 copy-done.1
  26.0 0.1 select_reduce_fusion.4
  26.1 0.3 select_reduce_fusion
  26.4 11.1 %all-to-all-done = bf16[8,8,4096]{2,0,1:T(8,128)(2,1)S(1)} async-done(((bf16[8,8,4096]{2,0,1:T(8,128)(2,1)}), bf16[8,8,4096]{2,0,1:T(8,128)(2,1)S(1)}, u32[]{:S(2)}, u32[]{:S(2)}) %all-to-all-start) | async-done | bytes 524320 | tf_op jit(solution)/shard_map/all_to_all | solution.py:27
  37.4 133.8 %all-reduce.3.cloned.1.call-done = (bf16[4096,256]{1,0:T(8,128)(2,1)}, bf16[4096,256]{1,0:T(8,128)(2,1)}, bf16[4096,256]{1,0:T(8,128)(2,1)}, bf16[4096,256]{1,0:T(8,128)(2,1)}) async-done(((bf16[4096,256]{1,0:T(8,128)(2,1)}, bf16[4096,256]{1,0:T(8,128)(2,1)}, bf16[4096,256]{1,0:T(8,128)(2,1)}, bf16[4096,256]{1,0:T(8,128)(2,1)}), (bf16[4096,256]{1,0:T(8,128)(2,1)}, bf16[4096,256]{1,0:T(8,128)(2,1)}, ...) | async-done | bytes 8388624 | tf_op jit(solution)/shard_map/psum | solution.py:11
  171.3 0.0 copy-start.5
  171.3 2.4 fusion.15
  173.7 0.0 copy-done.5
  173.7 0.0 copy-start.4
  173.7 0.8 fusion.14
  174.6 0.8 copy-done.4
  175.3 0.0 copy-start.3
  175.3 0.8 fusion.13
  176.1 0.8 copy-done.3
  176.9 0.8 fusion.12
  177.7 0.7 pad_maximum_fusion
  178.4 0.0 reduce-scatter.2.cloned.1.call-update
  178.5 62.7 %reduce-scatter.2.cloned.1.call-done = f32[8,1024]{1,0:T(8,128)} async-done(((f32[64,1024]{1,0:T(8,128)}), f32[8,1024]{1,0:T(8,128)}) %reduce-scatter.2.cloned.1.call-update) | async-done | bytes 32784 | tf_op jit(solution)/shard_map/reduce_scatter | solution.py:42
  241.2 1.4 convert_element_type.8
  (2 shorter events, 0.0 us)
Async XLA Ops:
  6.5 164.7 %all-reduce.3.cloned.1.call-start = ((), (), s32[]{:S(2)}) async-start(), calls=%async_computation.3 | async-start | bytes 16777216 | tf_op jit(solution)/shard_map/psum | solution.py:11
  15.5 10.1 %copy-start.2 = (s32[64]{0:T(128)S(1)}, s32[64]{0:T(128)}, u32[]{:S(2)}) copy-start(s32[64]{0:T(128)} %param.9) | copy-start | bytes 772
  15.5 10.3 %copy-start = (s32[1024]{0:T(1024)S(1)}, s32[1024]{0:T(1024)}, u32[]{:S(2)}) copy-start(s32[1024]{0:T(1024)} %param.10) | copy-start | bytes 12292
  15.5 10.5 %copy-start.1 = (s32[64]{0:T(128)S(1)}, s32[64]{0:T(128)}, u32[]{:S(2)}) copy-start(s32[64]{0:T(128)} %param.8) | copy-start | bytes 772
  15.5 21.9 %all-to-all-start = ((bf16[8,8,4096]{2,0,1:T(8,128)(2,1)}), bf16[8,8,4096]{2,0,1:T(8,128)(2,1)S(1)}, u32[]{:S(2)}, u32[]{:S(2)}) async-start(bf16[8,8,4096]{2,0,1:T(8,128)(2,1)} %bitcast.2), calls=%async_computation | async-start | bytes 1048576 | tf_op jit(solution)/shard_map/all_to_all | solution.py:27
  22.9 218.3 %reduce-scatter.2.cloned.1.call-start = ((), (), s32[]{:S(2)}) async-start(), calls=%async_computation.2 | async-start | bytes 294912 | tf_op jit(solution)/shard_map/reduce_scatter | solution.py:42
  171.3 2.4 copy-start.5
  173.7 1.6 copy-start.4
  175.3 1.6 copy-start.3
Sparse Core Ops, SparseCore 0:
  15.6 155.6 all-reduce.2
  178.6 62.5 reduce-scatter.1
where the time goes:
time: 250 us; the launch traced here: 249 us
  waiting for transfers between devices  208 us (83%)
  between operations  18.6 us (7%)
  other arithmetic  7.62 us (3%)
  starting transfers between devices  7.49 us (3%)
  matrix products  4.89 us (2%)
  local copies, waits for them, and re-layouts  3.18 us (1%)
    psum x1, waiting for transfers between devices, spread(): return lax.psum(kept, axis)  134 us
    reduce_scatter x1, waiting for transfers between devices, on_device(): lax.psum_scatter(jnp.concatenate([jnp.dot(transposed, masked, preferred_e...  62.7 us
    all_to_all x1, waiting for transfers between devices, on_device(): lax.all_to_all(amplitudes, 'wide', split_axis=1, concat_axis=0, tiled=True)  11.1 us
    all_to_all x1, starting transfers between devices, on_device(): lax.all_to_all(amplitudes, 'wide', split_axis=1, concat_axis=0, tiled=True)  7.45 us
  transfers between devices with their start and end apart: 3, of which 3 were waited for; matrix products, arithmetic and copies ran while one was open for 0% of the time, Pallas kernels for 0%

commit v1 on v0

--- a/solution.py
+++ b/solution.py
@@ -8,7 +8,7 @@
 
 def spread(value, axis, source):
     kept = jnp.where(lax.axis_index(axis) == source, value, 0).astype(value.dtype)
-    return lax.psum(kept, axis)
+    return jnp.sum(lax.all_gather(kept, axis), axis=0)
 
 
 def pair_irreps(window, block_irrep, block_units):

time: 250 us -> 340 us (1.36)
  waiting for transfers between devices: 208 us -> 273 us
  other arithmetic: 7.62 us -> 33.3 us
    all_gather x0 -> x4, waiting for transfers between devices: none -> 209 us  [spread(): return jnp.sum(lax.all_gather(kept, axis), axis=0)]
    psum x1 -> x0, waiting for transfers between devices: 134 us -> none  [spread(): return lax.psum(kept, axis)]
    reduce_sum x0 -> x4, other arithmetic: none -> 25.7 us  [spread(): return jnp.sum(lax.all_gather(kept, axis), axis=0)]
    all_to_all x1, waiting for transfers between devices: 11.1 us -> 0.01 us  [on_device(): lax.all_to_all(amplitudes, 'wide', split_axis=1, concat_axis=0, tiled=True)]
  transfers between devices with their start and end apart: 3 -> 6, of which waited for: 3 -> 5; matrix products, arithmetic and copies ran while one was open for 0% -> 8% of each run, Pallas kernels for 0% -> 0%
where the time goes in v1:
time: 340 us; the launch traced here: 339 us
  waiting for transfers between devices  273 us (80%)
  other arithmetic  33.3 us (10%)
  between operations  18.3 us (5%)
  starting transfers between devices  7.48 us (2%)
  local copies, waits for them, and re-layouts  3.94 us (1%)
    all_gather x4, waiting for transfers between devices, spread(): return jnp.sum(lax.all_gather(kept, axis), axis=0)  209 us
    reduce_scatter x1, waiting for transfers between devices, on_device(): lax.psum_scatter(jnp.concatenate([jnp.dot(transposed, masked, preferred_e...  62.6 us
    reduce_sum x4, other arithmetic, spread(): return jnp.sum(lax.all_gather(kept, axis), axis=0)  25.7 us
    all_to_all x1, starting transfers between devices, on_device(): lax.all_to_all(amplitudes, 'wide', split_axis=1, concat_axis=0, tiled=True)  7.32 us
  transfers between devices with their start and end apart: 6, of which 5 were waited for; matrix products, arithmetic and copies ran while one was open for 8% of the time, Pallas kernels for 0%

profile of v1, /device:TPU:0, one launch (start us, length us, event | category | flops | bytes accessed | tf_op | source)
XLA Modules:
  0.0 339.5 jit_solution(8980459849854023341)
XLA Ops:
  6.5 0.0 all-gather.15.cloned.1.call-start
  6.5 1.5 fusion.29
  10.5 4.9 %broadcast_select_fusion.3 = (bf16[4096,256]{1,0:T(8,128)(2,1)}, bf16[4096,256]{1,0:T(8,128)(2,1)}, bf16[4096,256]{1,0:T(8,128)(2,1)}, bf16[4096,256]{1,0:T(8,128)(2,1)}) fusion(bf16[4096,256]{1,0:T(8,128)(2,1)} %param.7, pred[]{:T(512)S(6)} %eq.29, pred[]{:T(512)S(6)} %eq.64, pred[]{:T(512)S(6)} %eq.70, pred[]{:T(512)S(6)} %eq.67), kind=kLoop, calls=%fused_computation.15 | loop fusion | flops 4194304 | bytes 10485764 | tf_op jit(solution)/shard_map/jit(_where)/select_n | solution.py:10
  15.4 0.0 all-gather.15.cloned.1.call-update
  15.5 0.0 all-gather.13.cloned.1.call-start
  15.5 0.7 all-gather.13.cloned.1.call-update
  16.2 0.0 all-gather.11.cloned.1.call-start
  16.3 0.7 all-gather.11.cloned.1.call-update
  16.9 0.0 copy-start.5
  17.0 0.0 copy-start.3
  17.0 0.0 copy-start.4
  17.0 0.0 all-gather.9.cloned.1.call-start
  17.0 0.5 all-gather.9.cloned.1.call-update
  17.6 7.3 %all-to-all-start = ((bf16[8,8,4096]{2,0,1:T(8,128)(2,1)}), bf16[8,8,4096]{2,0,1:T(8,128)(2,1)S(1)}, u32[]{:S(2)}, u32[]{:S(2)}) async-start(bf16[8,8,4096]{2,0,1:T(8,128)(2,1)} %bitcast.3), calls=%async_computation | async-start | bytes 1048576 | tf_op jit(solution)/shard_map/all_to_all | solution.py:27
  24.9 0.0 reduce-scatter.2.cloned.1.call-start
  27.4 0.0 copy-done.5
  27.4 0.1 copy.9
  27.5 0.1 reduce-window.7
  27.7 0.0 copy-done.3
  27.7 0.1 fusion.28
  27.8 0.1 multiply_reduce_fusion
  27.9 0.0 copy-done.4
  27.9 0.1 select_reduce_fusion.4
  28.0 0.3 select_reduce_fusion
  28.3 48.3 %all-gather.15.cloned.1.call-done = bf16[16384,256]{1,0:T(8,128)(2,1)} async-done(((bf16[4096,256]{1,0:T(8,128)(2,1)}), bf16[16384,256]{1,0:T(8,128)(2,1)}) %all-gather.15.cloned.1.call-update) | async-done | bytes 8388624 | tf_op jit(solution)/shard_map/all_gather | solution.py:11
  76.6 6.0 %reduce_sum.101 = bf16[4096,256]{1,0:T(8,128)(2,1)S(1)} reduce(bf16[4,4096,256]{2,1,0:T(8,128)(2,1)} %bitcast.29, bf16[]{:T(256)} %constant.33.clone.1), dimensions={0}, to_apply=%region_9.10 | reduce | flops 3145728 | bytes 10485762 | tf_op jit(solution)/shard_map/reduce_sum | solution.py:11
  82.6 53.8 %all-gather.13.cloned.1.call-done = bf16[16384,256]{1,0:T(8,128)(2,1)} async-done(((bf16[4096,256]{1,0:T(8,128)(2,1)}), bf16[16384,256]{1,0:T(8,128)(2,1)}) %all-gather.13.cloned.1.call-update) | async-done | bytes 8388624 | tf_op jit(solution)/shard_map/all_gather | solution.py:11
  136.5 6.6 %reduce_sum.99 = bf16[4096,256]{1,0:T(8,128)(2,1)} reduce(bf16[4,4096,256]{2,1,0:T(8,128)(2,1)} %bitcast.30, bf16[]{:T(256)} %constant.33.clone.1), dimensions={0}, to_apply=%region_7.8 | reduce | flops 3145728 | bytes 10485762 | tf_op jit(solution)/shard_map/reduce_sum | solution.py:11
  143.1 53.3 %all-gather.11.cloned.1.call-done = bf16[16384,256]{1,0:T(8,128)(2,1)} async-done(((bf16[4096,256]{1,0:T(8,128)(2,1)}), bf16[16384,256]{1,0:T(8,128)(2,1)}) %all-gather.11.cloned.1.call-update) | async-done | bytes 8388624 | tf_op jit(solution)/shard_map/all_gather | solution.py:11
  196.3 6.5 %reduce_sum.97 = bf16[4096,256]{1,0:T(8,128)(2,1)} reduce(bf16[4,4096,256]{2,1,0:T(8,128)(2,1)} %bitcast.31, bf16[]{:T(256)} %constant.33.clone.1), dimensions={0}, to_apply=%region_5.6 | reduce | flops 3145728 | bytes 10485762 | tf_op jit(solution)/shard_map/reduce_sum | solution.py:11
  202.8 53.2 %all-gather.9.cloned.1.call-done = bf16[16384,256]{1,0:T(8,128)(2,1)} async-done(((bf16[4096,256]{1,0:T(8,128)(2,1)}), bf16[16384,256]{1,0:T(8,128)(2,1)}) %all-gather.9.cloned.1.call-update) | async-done | bytes 8388624 | tf_op jit(solution)/shard_map/all_gather | solution.py:11
  256.0 6.6 %reduce_sum.95 = bf16[4096,256]{1,0:T(8,128)(2,1)} reduce(bf16[4,4096,256]{2,1,0:T(8,128)(2,1)} %bitcast.32, bf16[]{:T(256)} %constant.33.clone.1), dimensions={0}, to_apply=%region_3.4 | reduce | flops 3145728 | bytes 10485762 | tf_op jit(solution)/shard_map/reduce_sum | solution.py:11
  262.6 0.0 all-to-all-done
  262.6 0.0 copy-start
  262.6 0.8 fusion.12
  263.5 0.8 copy-done
  264.2 0.0 copy-start.1
  264.2 0.8 fusion.13
  265.1 0.8 copy-done.1
  265.8 0.0 copy-start.2
  265.8 0.8 fusion.14
  266.6 0.8 copy-done.2
  267.4 0.8 fusion.15
  268.2 0.7 pad_maximum_fusion
  268.9 0.0 reduce-scatter.2.cloned.1.call-update
  269.0 62.6 %reduce-scatter.2.cloned.1.call-done = f32[8,1024]{1,0:T(8,128)} async-done(((f32[64,1024]{1,0:T(8,128)}), f32[8,1024]{1,0:T(8,128)}) %reduce-scatter.2.cloned.1.call-update) | async-done | bytes 32784 | tf_op jit(solution)/shard_map/reduce_scatter | solution.py:42
  331.6 1.4 convert_element_type.7
  (2 shorter events, 0.0 us)
Async XLA Ops:
  6.5 70.1 %all-gather.15.cloned.1.call-start = ((), (), s32[]{:S(2)}) async-start(), calls=%async_computation.6 | async-start | bytes 10485760 | tf_op jit(solution)/shard_map/all_gather | solution.py:11
  15.5 121.0 %all-gather.13.cloned.1.call-start = ((), (), s32[]{:S(2)}) async-start(), calls=%async_computation.5 | async-start | bytes 10485760 | tf_op jit(solution)/shard_map/all_gather | solution.py:11
  16.2 180.1 %all-gather.11.cloned.1.call-start = ((), (), s32[]{:S(2)}) async-start(), calls=%async_computation.4 | async-start | bytes 10485760 | tf_op jit(solution)/shard_map/all_gather | solution.py:11
  16.9 10.5 %copy-start.5 = (s32[64]{0:T(128)S(1)}, s32[64]{0:T(128)}, u32[]{:S(2)}) copy-start(s32[64]{0:T(128)} %param.9) | copy-start | bytes 772
  17.0 10.7 %copy-start.3 = (s32[1024]{0:T(1024)S(1)}, s32[1024]{0:T(1024)}, u32[]{:S(2)}) copy-start(s32[1024]{0:T(1024)} %param.10) | copy-start | bytes 12292
  17.0 10.9 %copy-start.4 = (s32[64]{0:T(128)S(1)}, s32[64]{0:T(128)}, u32[]{:S(2)}) copy-start(s32[64]{0:T(128)} %param.8) | copy-start | bytes 772
  17.0 239.1 %all-gather.9.cloned.1.call-start = ((), (), s32[]{:S(2)}) async-start(), calls=%async_computation.3 | async-start | bytes 10485760 | tf_op jit(solution)/shard_map/all_gather | solution.py:11
  17.6 245.1 %all-to-all-start = ((bf16[8,8,4096]{2,0,1:T(8,128)(2,1)}), bf16[8,8,4096]{2,0,1:T(8,128)(2,1)S(1)}, u32[]{:S(2)}, u32[]{:S(2)}) async-start(bf16[8,8,4096]{2,0,1:T(8,128)(2,1)} %bitcast.3), calls=%async_computation | async-start | bytes 1048576 | tf_op jit(solution)/shard_map/all_to_all | solution.py:27
  24.9 306.7 %reduce-scatter.2.cloned.1.call-start = ((), (), s32[]{:S(2)}) async-start(), calls=%async_computation.2 | async-start | bytes 294912 | tf_op jit(solution)/shard_map/reduce_scatter | solution.py:42
  262.6 1.6 copy-start
  264.2 1.6 copy-start.1
  265.8 1.6 copy-start.2
Sparse Core Ops, SparseCore 0:
  15.6 60.9 all-gather.14
  78.2 58.2 all-gather.12
  138.0 58.2 all-gather.10
  197.7 58.2 all-gather.8
  269.1 62.4 reduce-scatter.1
